TPU v7x, 32 devices: a whole 2x2x4 slice. The times are simulated.
32 devices in a mesh: grp: 2 (over x), row: 16 (over z, y, core).
Axes of the slice: x: 2, y: 2, z: 4, core: 2. Of those that a mesh axis runs over, the one named last changes fastest.
Arguments:
- aligned_sequences: bfloat16 [32, 64, 64], P(None, ('grp', 'row')), parts along dimension 1, may hold values from -6 to 6
- first_factor_matrix: bfloat16 [64, 32], replicated, may hold values from -0.75 to 0.75
- second_factor_matrix: bfloat16 [64, 32], replicated, may hold values from -0.75 to 0.75
- tensor_matrix: bfloat16 [1024, 128], replicated, may hold values from -1 to 1
- tensor_offset: bfloat16 [128], replicated, may hold values from -4 to 4
- structural_duplex_patches: bfloat16 [512, 2048], P(('grp', 'row')), parts along dimension 0, may hold values from -6 to 6
- patch_source_index: int32 [512, 1], P(('grp', 'row')), parts along dimension 0, may hold values from 0 to 15; in each aligned block of 16 rows (0 to 15, 16 to 31, ...) at most 2 rows name the same one
- patch_target_index: int32 [512], P(('grp', 'row')), parts along dimension 0, may hold values from 0 to 1
- structural_matrix: bfloat16 [64, 128], replicated, may hold values from -0.75 to 0.75
- polymer_residue_lengths: int32 [16], P('grp'), parts along dimension 0, may hold values from 1 to 16, 32 in all
- sigmoid_matrix: bfloat16 [128, 128], replicated, may hold values from -0.5 to 0.5
- content_matrix: bfloat16 [128, 128], replicated, may hold values from -0.5 to 0.5
Outputs:
- update: bfloat16 [64, 32, 128], P(('grp', 'row')), parts along dimension 0
There are 2 independent parts, one for each index of `grp`. A program takes and returns all parts, laid end to end along the dimension named above; an argument that names none is the same for every part. Nothing has to cross between parts.
Inputs may be any that keep to these rules, and one draw needn't show every extreme that they name: `patch_source_index`: among the tiles of one device no owner is named more than 2 times, a bound that some block reaches.
All inputs are finite; a program needn't handle non-finite values.
Results may differ from a plain program's by a relative error of at most 0.0073.
Values may be sent and summed in bfloat16 or wider, within the bound.
No kernel may reach another device: no remote copies, remote signals or barrier semaphores. Data moves between devices by JAX's collectives and lax.ppermute only.
A program may use at most 64 MiB of HBM per device.

v0:
```python
import functools
import math

import jax
import jax.numpy as jnp
from jax import lax
from jax.experimental import pallas as pl
from jax.experimental.pallas import tpu as pltpu
from jax.sharding import PartitionSpec as P

CAP = 2
LANES = 128
ORDERS = {16: (8, 3, 5, 2, 15, 7, 12, 4, 14, 13, 10, 1, 6, 11, 0, 9)}
VMEM = pltpu.MemorySpace.VMEM
HBM = pltpu.MemorySpace.HBM


def dot(a, b):
    return jnp.dot(a, b, preferred_element_type=jnp.float32)


def dot_nt(a, b):
    return lax.dot_general(a, b, (((1,), (1,)), ((), ())), preferred_element_type=jnp.float32)


def exchange_order(n_devices):
    return ORDERS.get(n_devices, tuple(range(n_devices)))


def store_rows(ref, places, value):
    step = places[1] - places[0]
    if step > 0 and all(b - a == step for a, b in zip(places, places[1:])):
        ref[pl.ds(places[0], len(places), stride=step), :] = value
    else:
        for n, place in enumerate(places):
            ref[pl.ds(place, 1), :] = value[n : n + 1]


def standardize(x):
    centred = x - jnp.mean(x, axis=-1, keepdims=True)
    variance = jnp.mean(centred * centred, axis=-1, keepdims=True)
    return centred * lax.rsqrt(variance + 1e-05)


def pack_kernel(n_devices, rows, tc, n_loads, *refs):
    (
        x_hbm,
        second_hbm,
        tiles_hbm,
        owner_hbm,
        column_hbm,
        first_hbm,
        lengths_hbm,
        tensor_hbm,
        offset_hbm,
        structural_hbm,
        sigmoid_hbm,
        content_hbm,
        send_ref,
        left_ref,
        same_ref,
        tensor_ref,
        offset_ref,
        structural_ref,
        sigmoid_ref,
        content_ref,
        x_ref,
        second_ref,
        tiles_ref,
        owner_ref,
        column_ref,
        first_ref,
        lengths_ref,
        wide,
        arrived,
    ) = refs
    pairs = tensor_ref.shape[0]
    copies = [
        (owner_hbm, owner_ref),
        (column_hbm, column_ref),
        (x_hbm, x_ref),
        (second_hbm, second_ref),
        (tiles_hbm, tiles_ref),
        (lengths_hbm, lengths_ref),
        (first_hbm, first_ref),
        (offset_hbm, offset_ref),
        (structural_hbm, structural_ref),
        (sigmoid_hbm, sigmoid_ref),
        (content_hbm, content_ref),
    ] + [(tensor_hbm.at[:, p], tensor_ref.at[p]) for p in range(pairs)]
    loads = [pltpu.make_async_copy(source, target, arrived.at[n]) for n, (source, target) in enumerate(copies)]
    for load in loads:
        load.start()
    depth, lines, _ = x_ref.shape
    slots, width = tiles_ref.shape
    tile_rows = width // LANES
    n_chan = second_ref.shape[0]
    right_rows = n_chan * depth // LANES
    base = lines * right_rows
    here = lax.broadcasted_iota(jnp.int32, (slots, slots), 0)
    there = lax.broadcasted_iota(jnp.int32, (slots, slots), 1)
    order = exchange_order(n_devices)
    slot = lax.broadcasted_iota(jnp.int32, (CAP * n_devices, slots), 0)
    if order != tuple(range(n_devices)):
        position = slot % n_devices
        device = jnp.zeros_like(slot)
        for p, d in enumerate(order):
            device = jnp.where(position == p, d, device)
        slot = slot - position + device
    spread_row = lax.broadcasted_iota(jnp.int32, (4 * n_chan, n_chan), 0)
    spread_chan = lax.broadcasted_iota(jnp.int32, (4 * n_chan, n_chan), 1)
    parity = spread_row // (2 * n_chan)
    spread = ((spread_row - parity * 2 * n_chan) == spread_chan * 2 + parity).astype(jnp.bfloat16)
    for load in loads[:5]:
        load.wait()
    across = jnp.broadcast_to(owner_ref[...], (slots, slots))
    down = jnp.sum(jnp.where(here == there, across, 0), axis=1, keepdims=True)
    rank = jnp.sum(jnp.where((down == across) & (here < there), 1, 0), axis=0, keepdims=True)
    target = rank * n_devices + owner_ref[...]
    place = slot == target
    code = jnp.where(place, (column_ref[...] + 1).astype(jnp.float32), 0.0)
    code = jnp.broadcast_to(jnp.sum(code, axis=1, keepdims=True), (CAP * n_devices, LANES))
    for c in range(CAP):
        wide[pl.ds(base + CAP * tile_rows + c, n_devices, stride=rows), :] = code[
            c * n_devices : (c + 1) * n_devices
        ]
    x = x_ref[...].astype(jnp.float32)
    normed = []
    for t in range(lines):
        normed.append(standardize(x[:, t, :]).astype(jnp.bfloat16))
        right = dot_nt(second_ref[...], normed[t])
        groups = n_chan // right_rows
        packed = jnp.concatenate(
            [right[b * right_rows : (b + 1) * right_rows] for b in range(groups)], axis=1
        )
        for d in range(n_devices):
            wide[pl.ds(d * rows + t * right_rows, right_rows), :] = packed
    place = place.astype(jnp.bfloat16)
    for q in range(tile_rows):
        placed = dot(place, tiles_ref[:, q * LANES : (q + 1) * LANES])
        for c in range(CAP):
            wide[pl.ds(base + c * tile_rows + q, n_devices, stride=rows), :] = placed[
                c * n_devices : (c + 1) * n_devices
            ]
    send_ref[...] = wide[...].astype(jnp.bfloat16)

    for load in loads[5:7]:
        load.wait()
    first = dot(spread, first_ref[...]).astype(jnp.bfloat16)
    for t in range(lines):
        left = dot_nt(normed[t], first).astype(jnp.bfloat16).astype(jnp.float32)
        left_ref[pl.ds(t * depth, depth), :] = (left * (1.0 / depth)).astype(jnp.bfloat16)
    per_row = tile_rows // lines
    packed = tc // per_row
    row = lax.broadcasted_iota(jnp.int32, same_ref.shape, 0)
    lane = lax.broadcasted_iota(jnp.int32, same_ref.shape, 1)
    column = (row // tile_rows) * tc + (row % per_row) * packed + lane // (LANES // packed)
    line = lax.axis_index("row") * lines + (row % tile_rows) // per_row
    end = jnp.int32(0)
    column_chain = jnp.zeros_like(column)
    line_chain = jnp.zeros_like(line)
    for c in range(lengths_ref.shape[0]):
        end = end + lengths_ref[c]
        column_chain = column_chain + (column >= end).astype(jnp.int32)
        line_chain = line_chain + (line >= end).astype(jnp.int32)
    same_ref[...] = (column_chain == line_chain).astype(jnp.float32)
    for load in loads[7:]:
        load.wait()


def pair_kernel(
    n_devices,
    rows,
    tc,
    got_ref,
    left_ref,
    same_ref,
    tensor_ref,
    offset_ref,
    structural_ref,
    sigmoid_ref,
    content_ref,
    out_ref,
    folded,
    wide,
    sums,
    pair,
    opm,
):
    n_temp, pair_chan = structural_ref.shape
    lines = folded.shape[1] // pair_chan
    right_rows = folded.shape[0] // LANES
    depth = left_ref.shape[0] // lines
    n_tokens = n_devices * lines
    n_tiles = n_tokens // tc
    tile_rows = same_ref.shape[0] // n_tiles
    base = lines * right_rows

    width = left_ref.shape[1] // 2
    for p in range(tensor_ref.shape[0] // width):
        for parity in range(2):
            part = dot(
                left_ref[:, parity * width : (parity + 1) * width], tensor_ref[pl.ds(p * width, width), :]
            ).astype(jnp.bfloat16)
            d = 2 * p + parity
            at = (d % right_rows) * LANES + (d // right_rows) * depth
            for t in range(lines):
                folded[pl.ds(at, depth), t * pair_chan : (t + 1) * pair_chan] = part[t * depth : (t + 1) * depth]

    wide[...] = got_ref[...].astype(jnp.float32)

    unrolled = n_devices <= 16
    if not unrolled:
        sums[...] = jnp.zeros_like(sums)

    def add_source(d, carry):
        start = d * rows
        counts, totals = carry
        for c in range(CAP):
            tile = wide[pl.ds(start + base + c * tile_rows, tile_rows), :]
            code = wide[pl.ds(start + base + CAP * tile_rows + c, 1), :]
            for k in range(n_tiles):
                hit = code == k + 1.0
                counts[k] = counts[k] + jnp.where(hit, 1.0, 0.0)
                term = jnp.where(hit, tile, 0.0)
                if unrolled:
                    totals[k] = term if totals[k] is None else totals[k] + term
                else:
                    at = pl.ds(k * tile_rows, tile_rows)
                    sums[at, :] = sums[at, :] + term
        return counts, totals

    counts = [jnp.zeros((1, LANES), jnp.float32) for _ in range(n_tiles)]
    totals = [None] * n_tiles
    if unrolled:
        for d in range(n_devices):
            counts, totals = add_source(d, (counts, totals))
    else:
        counts = lax.fori_loop(0, n_devices, lambda d, kept: add_source(d, (kept, totals))[0], counts)
        totals = [sums[pl.ds(k * tile_rows, tile_rows), :] for k in range(n_tiles)]
    outer = None
    for g in range(right_rows):
        lhs = jnp.concatenate(
            [wide[pl.ds(t * right_rows + g, n_devices, stride=rows), :] for t in range(lines)], axis=0
        ).astype(jnp.bfloat16)
        term = dot(lhs, folded[pl.ds(g * LANES, LANES), :])
        outer = term if outer is None else outer + term
    order = exchange_order(n_devices)
    for i in range(lines):
        for t in range(lines):
            store_rows(
                opm,
                [i * n_tokens + d * lines + t for d in order],
                outer[t * n_devices : (t + 1) * n_devices, i * pair_chan : (i + 1) * pair_chan],
            )
    packed = LANES // n_temp
    per_row = tile_rows // lines
    for k in range(n_tiles):
        at = pl.ds(k * tile_rows, tile_rows)
        mean = totals[k] / jnp.maximum(counts[k], 1.0)
        template = (mean * same_ref[at, :]).astype(jnp.bfloat16)
        for h in range(packed):
            part = dot(template[:, h * n_temp : (h + 1) * n_temp], structural_ref[...])
            for i in range(lines):
                first = i * n_tokens + k * tc + h
                pair[pl.ds(first, per_row, stride=packed), :] = part[i * per_row : (i + 1) * per_row]
    for i in range(lines):
        at = pl.ds(i * n_tokens, n_tokens)
        total = pair[at, :] + (opm[at, :] + offset_ref[...].astype(jnp.float32))
        pair_normed = standardize(total).astype(jnp.bfloat16)
        gate = jax.nn.sigmoid(dot(pair_normed, sigmoid_ref[...]))
        linear = dot(pair_normed, content_ref[...])
        out_ref[at, :] = (gate * linear).astype(out_ref.dtype)


def grant(*arrays):
    return pltpu.CompilerParams(
        vmem_limit_bytes=sum(2 * math.prod(shape) * jnp.dtype(kind).itemsize for shape, kind in arrays) + (1 << 20)
    )


def on_device(
    aligned_sequences,
    first_factor_matrix,
    second_factor_matrix,
    tensor_matrix,
    tensor_offset,
    structural_duplex_patches,
    patch_source_index,
    patch_target_index,
    structural_matrix,
    polymer_residue_lengths,
    sigmoid_matrix,
    content_matrix,
):
    n_devices = lax.axis_size("row")
    depth, lines, n_feat = aligned_sequences.shape
    slots, width = structural_duplex_patches.shape
    n_chan = first_factor_matrix.shape[1]
    n_temp, pair_chan = structural_matrix.shape
    tc = width // (lines * n_temp)
    n_tokens = lines * n_devices
    n_tiles = n_tokens // tc
    tile_rows = width // LANES
    right_rows = n_chan * depth // LANES
    rows = lines * right_rows + CAP * tile_rows + CAP
    vmem = pl.BlockSpec(memory_space=VMEM)
    hbm = pl.BlockSpec(memory_space=HBM)
    half = n_chan // 2
    f32, bf16, i32 = jnp.float32, jnp.bfloat16, jnp.int32

    arguments = (
        aligned_sequences,
        second_factor_matrix.T,
        structural_duplex_patches,
        patch_source_index.reshape(1, slots),
        patch_target_index.reshape(1, slots),
        first_factor_matrix.T,
        polymer_residue_lengths,
        tensor_matrix.reshape(n_chan, half, 2, pair_chan),
        tensor_offset.reshape(1, pair_chan),
        structural_matrix,
        sigmoid_matrix,
        content_matrix,
    )
    results = (
        ((n_devices * rows, LANES), bf16),
        ((lines * depth, 4 * n_chan), bf16),
        ((n_tiles * tile_rows, LANES), f32),
        ((half, n_chan, 2, pair_chan), bf16),
        ((1, pair_chan), bf16),
        (structural_matrix.shape, bf16),
        (sigmoid_matrix.shape, bf16),
        (content_matrix.shape, bf16),
    )
    scratch = (
        (aligned_sequences.shape, bf16),
        ((n_chan, n_feat), bf16),
        ((slots, width), bf16),
        ((1, slots), i32),
        ((1, slots), i32),
        ((n_chan, n_feat), bf16),
    )
    packed_wide = ((n_devices * rows, LANES), f32)
    n_loads = 11 + half
    send, left, same, tensor, offset, structural, sigmoid, content = pl.pallas_call(
        functools.partial(pack_kernel, n_devices, rows, tc, n_loads),
        out_shape=[jax.ShapeDtypeStruct(*r) for r in results],
        in_specs=[hbm] * len(arguments),
        out_specs=[vmem] * len(results),
        scratch_shapes=[pltpu.VMEM(*a) for a in scratch]
        + [pltpu.SMEM(polymer_residue_lengths.shape, i32), pltpu.VMEM(*packed_wide)]
        + [pltpu.SemaphoreType.DMA((n_loads,))],
        compiler_params=grant(*results, *scratch, packed_wide),
    )(*(pltpu.with_memory_space_constraint(a, HBM) for a in arguments))
    got = lax.all_to_all(
        send.reshape(n_devices, rows // 2, 2, LANES),
        "row",
        split_axis=0,
        concat_axis=0,
        tiled=True,
        axis_index_groups=[exchange_order(n_devices)],
    ).reshape(n_devices * rows, LANES)
    tensor = tensor.reshape(n_chan * n_chan, pair_chan)
    scratch = (
        ((n_chan * depth, lines * pair_chan), bf16),
        packed_wide,
        ((n_tiles * tile_rows, LANES), f32),
        ((lines * n_tokens, pair_chan), f32),
        ((lines * n_tokens, pair_chan), f32),
    )
    result = ((lines * n_tokens, pair_chan), bf16)
    out = pl.pallas_call(
        functools.partial(pair_kernel, n_devices, rows, tc),
        out_shape=jax.ShapeDtypeStruct(*result),
        in_specs=[vmem] * 8,
        out_specs=vmem,
        scratch_shapes=[pltpu.VMEM(*a) for a in scratch],
        compiler_params=grant(*results, *scratch, result),
    )(got, left, same, tensor, offset, structural, sigmoid, content)
    return out.reshape(lines, n_tokens, pair_chan)


def solution(mesh):
    placed = (
        P(None, ("grp", "row"), None),
        P(),
        P(),
        P(),
        P(),
        P(("grp", "row"), None),
        P(("grp", "row"), None),
        P(("grp", "row")),
        P(),
        P("grp"),
        P(),
        P(),
    )
    return jax.shard_map(
        on_device,
        mesh=mesh,
        in_specs=placed,
        out_specs=P(("grp", "row"), None, None),
        check_vma=False,
    )
```

profile of v0, /device:TPU:0, one launch (start us, length us, event | category | flops | bytes accessed | tf_op | source)
XLA Modules:
  0.0 15.8 jit_solution(15419940861691691988)
XLA Ops:
  0.0 1.9 %shard_map.118 = (bf16[800,128]{1,0:T(8,128)(2,1)S(1)}, bf16[64,128]{1,0:T(8,128)(2,1)S(1)}, f32[32,128]{1,0:T(8,128)S(1)}, bf16[16,32,2,128]{3,2,1,0:T(2,128)(2...) custom-call(bf16[32,2,64]{2,1,0:T(2,128)(2,1)} %refs_0_.1, ...), custom_call_target="tpu_custom_call" | custom-call | tf_op jit(solution)/shard_map/pallas_call | solution.py:346
  1.9 12.4 %all_to_all.5 = bf16[16,25,2,128]{3,2,1,0:T(2,128)(2,1)S(1)} all-to-all(bf16[16,25,2,128]{3,2,1,0:T(2,128)(2,1)S(1)} %bitcast.12), channel_id=1, replica_groups={{8,3,5,2,15,7,12,4,14,13,10,1,6,11,0,9},{24,19,21,18,31,23,28,20,30,29,..., dimensions={0} | all-to-all | bytes 409600 | tf_op jit(solution)/shard_map/all_to_all | solution.py:356
  14.3 1.5 %shard_map.119 = bf16[64,128]{1,0:T(8,128)(2,1)} custom-call(bf16[800,128]{1,0:T(8,128)(2,1)S(1)} %bitcast.10, bf16[64,128]{1,0:T(8,128)(2,1)S(1)} %get-tuple-element.14.left_ref, f32[32,128]{1,0:T(8,128)S(1)} %get-tuple-element.15.same_ref, bf16[1024,128]{1,0:T(8,128)(2,1)S(1)} %bitcast.11, bf16[1,128]{1,0:T(2,128)(2,1)S(1)} %get-tuple-element.17.offset_ref, ...), custom_call_target="tpu_custom_call" | custom-call | tf_op jit(solution)/shard_map/pallas_call | solution.py:373
where the time goes:
time: 16.1 us; the launch traced here: 15.8 us
  blocking collectives  12.4 us (77%)
  Pallas kernels  3.37 us (21%)
    all_to_all x1, blocking collectives, on_device(): lax.all_to_all(send.reshape(n_devices, rows // 2, 2, LANES), 'row', split...  12.4 us
    pallas_call x1, Pallas kernels, on_device(): pl.pallas_call(functools.partial(pack_kernel, n_devices, rows, tc, n_load...  1.88 us
    pallas_call x1, Pallas kernels, on_device(): pl.pallas_call(functools.partial(pair_kernel, n_devices, rows, tc), out_s...  1.49 us

commit v1 on v0

v1 whole, which is shorter than its diff:
```python
import functools
import math

import jax
import jax.numpy as jnp
from jax import lax
from jax.experimental import pallas as pl
from jax.experimental.pallas import tpu as pltpu
from jax.sharding import PartitionSpec as P

CAP = 2
LANES = 128
ORDERS = {16: (8, 3, 5, 2, 15, 7, 12, 4, 14, 13, 10, 1, 6, 11, 0, 9)}
VMEM = pltpu.MemorySpace.VMEM
HBM = pltpu.MemorySpace.HBM


def dot(a, b):
    return jnp.dot(a, b, preferred_element_type=jnp.float32)


def dot_nt(a, b):
    return lax.dot_general(a, b, (((1,), (1,)), ((), ())), preferred_element_type=jnp.float32)


def exchange_order(n_devices):
    return ORDERS.get(n_devices, tuple(range(n_devices)))


def standardize(x):
    centred = x - jnp.mean(x, axis=-1, keepdims=True)
    variance = jnp.mean(centred * centred, axis=-1, keepdims=True)
    return centred * lax.rsqrt(variance + 1e-05)


def pack_kernel(n_devices, lines, rows, tc, *refs):
    (
        x_hbm,
        second_hbm,
        tiles_hbm,
        owner_hbm,
        column_hbm,
        first_hbm,
        lengths_hbm,
        tensor_hbm,
        offset_hbm,
        structural_hbm,
        sigmoid_hbm,
        content_hbm,
        send_ref,
        left_ref,
        same_ref,
        tensor_ref,
        offset_ref,
        weights_ref,
        features_ref,
        tiles_ref,
        index_ref,
        lengths_ref,
        normed_ref,
        wide,
        arrived,
    ) = refs

    def load(n, target, *sources):
        at = 0
        for source in sources:
            size = source.shape[0]
            pltpu.make_async_copy(source, target.at[pl.ds(at, size)], arrived.at[n]).start()
            at = at + size
        return pltpu.make_async_copy(target, target, arrived.at[n])

    index_load = load(0, index_ref, owner_hbm, column_hbm)
    features_load = load(1, features_ref, x_hbm, second_hbm, first_hbm)
    tiles_load = load(2, tiles_ref, tiles_hbm)
    lengths_load = pltpu.make_async_copy(lengths_hbm, lengths_ref, arrived.at[3])
    lengths_load.start()
    offset_load = load(4, offset_ref, offset_hbm)
    weights_load = load(5, weights_ref, structural_hbm, sigmoid_hbm, content_hbm)
    for p in range(tensor_ref.shape[0]):
        pltpu.make_async_copy(tensor_hbm.at[:, p], tensor_ref.at[p], arrived.at[6]).start()
    tensor_load = pltpu.make_async_copy(tensor_ref, tensor_ref, arrived.at[6])
    slots, width = tiles_ref.shape
    depth = left_ref.shape[0] // (2 * lines)
    tile_rows = width // LANES
    n_chan = second_hbm.shape[0]
    right_rows = n_chan * depth // LANES
    base = lines * right_rows
    per_row = tile_rows // lines
    packed = tc // per_row
    row = lax.broadcasted_iota(jnp.int32, same_ref.shape, 0)
    lane = lax.broadcasted_iota(jnp.int32, same_ref.shape, 1)
    column = (row // tile_rows) * tc + (row % per_row) * packed + lane // (LANES // packed)
    line = (row % tile_rows) // per_row
    here = lax.broadcasted_iota(jnp.int32, (slots, slots), 0)
    there = lax.broadcasted_iota(jnp.int32, (slots, slots), 1)
    order = exchange_order(n_devices)
    slot = lax.broadcasted_iota(jnp.int32, (CAP * n_devices, slots), 0)
    if order != tuple(range(n_devices)):
        position = slot % n_devices
        device = jnp.zeros_like(slot)
        for p, d in enumerate(order):
            device = jnp.where(position == p, d, device)
        slot = slot - position + device
    spread_row = lax.broadcasted_iota(jnp.int32, (4 * n_chan, n_chan), 0)
    spread_chan = lax.broadcasted_iota(jnp.int32, (4 * n_chan, n_chan), 1)
    parity = spread_row // (2 * n_chan)
    spread = ((spread_row - parity * 2 * n_chan) == spread_chan * 2 + parity).astype(jnp.bfloat16)
    index_load.wait()
    features_load.wait()
    lengths_load.wait()
    tiles_load.wait()
    owner = index_ref[pl.ds(0, 1), :]
    across = jnp.broadcast_to(owner, (slots, slots))
    down = jnp.sum(jnp.where(here == there, across, 0), axis=1, keepdims=True)
    rank = jnp.sum(jnp.where((down == across) & (here < there), 1, 0), axis=0, keepdims=True)
    target = rank * n_devices + owner
    place = slot == target
    code = jnp.where(place, (index_ref[pl.ds(1, 1), :] + 1).astype(jnp.float32), 0.0)
    code = jnp.broadcast_to(jnp.sum(code, axis=1, keepdims=True), (CAP * n_devices, LANES))
    for c in range(CAP):
        wide[pl.ds(base + CAP * tile_rows + c, n_devices, stride=rows), :] = code[
            c * n_devices : (c + 1) * n_devices
        ]
    height = lines * depth
    normed_ref[...] = standardize(features_ref[pl.ds(0, height), :].astype(jnp.float32))
    second = features_ref[pl.ds(height, n_chan), :]
    first = dot(spread, features_ref[pl.ds(height + n_chan, n_chan), :]).astype(jnp.bfloat16)
    groups = n_chan // right_rows
    for t in range(lines):
        normed = normed_ref[pl.ds(t, depth, stride=lines), :].astype(jnp.bfloat16)
        right = dot_nt(second, normed)
        right = jnp.concatenate(
            [right[b * right_rows : (b + 1) * right_rows] for b in range(groups)], axis=1
        )
        for d in range(n_devices):
            wide[pl.ds(d * rows + t * right_rows, right_rows), :] = right
        for parity in range(2):
            left = dot_nt(normed, first[parity * 2 * n_chan : (parity + 1) * 2 * n_chan])
            left = left.astype(jnp.bfloat16).astype(jnp.float32) * (1.0 / depth)
            left_ref[pl.ds((parity * lines + t) * depth, depth), :] = left.astype(jnp.bfloat16)
    place = place.astype(jnp.bfloat16)
    for q in range(tile_rows):
        placed = dot(place, tiles_ref[:, q * LANES : (q + 1) * LANES])
        for c in range(CAP):
            wide[pl.ds(base + c * tile_rows + q, n_devices, stride=rows), :] = placed[
                c * n_devices : (c + 1) * n_devices
            ]
    low = jnp.zeros_like(column)
    high = jnp.zeros_like(column)
    for i in range(lines):
        token = lax.axis_index("row") * lines + i
        end, below, above = jnp.int32(0), jnp.int32(0), jnp.int32(2**31 - 1)
        for c in range(lengths_ref.shape[0]):
            end = end + lengths_ref[c]
            below = jnp.where(end <= token, jnp.maximum(below, end), below)
            above = jnp.where(end <= token, above, jnp.minimum(above, end))
        low = jnp.where(line == i, below, low)
        high = jnp.where(line == i, above, high)
    same_ref[...] = ((column >= low) & (column < high)).astype(jnp.float32)
    send_ref[...] = wide[...].astype(jnp.bfloat16)
    offset_load.wait()
    weights_load.wait()
    tensor_load.wait()


def pair_kernel(
    n_devices,
    rows,
    tc,
    got_ref,
    left_ref,
    same_ref,
    tensor_ref,
    offset_ref,
    weights_ref,
    out_ref,
    folded,
    wide,
    sums,
    pair,
    opm,
):
    pair_chan = weights_ref.shape[1]
    n_temp = weights_ref.shape[0] - 2 * pair_chan
    structural = weights_ref[pl.ds(0, n_temp), :]
    sigmoid = weights_ref[pl.ds(n_temp, pair_chan), :]
    content = weights_ref[pl.ds(n_temp + pair_chan, pair_chan), :]
    lines = folded.shape[1] // pair_chan
    right_rows = folded.shape[0] // LANES
    depth = left_ref.shape[0] // (2 * lines)
    n_tokens = n_devices * lines
    n_tiles = n_tokens // tc
    tile_rows = same_ref.shape[0] // n_tiles
    base = lines * right_rows

    width = left_ref.shape[1]
    for p in range(0, tensor_ref.shape[0] // width, 2):
        both = jnp.concatenate(
            [tensor_ref[pl.ds(p * width, width), :], tensor_ref[pl.ds((p + 1) * width, width), :]], axis=1
        )
        part = dot(left_ref[...], both).astype(jnp.bfloat16)
        for n in range(2):
            for parity in range(2):
                d = 2 * (p + n) + parity
                at = (d % right_rows) * LANES + (d // right_rows) * depth
                for t in range(lines):
                    first = (parity * lines + t) * depth
                    folded[pl.ds(at, depth), t * pair_chan : (t + 1) * pair_chan] = part[
                        first : first + depth, n * pair_chan : (n + 1) * pair_chan
                    ]

    wide[...] = got_ref[...].astype(jnp.float32)
    few = min(n_devices, 16)
    slots = few * CAP
    span = slots * tile_rows
    kept = n_tiles * tile_rows
    slot_of = lax.broadcasted_iota(jnp.int32, (slots, span), 1) // tile_rows
    slot_is = lax.broadcasted_iota(jnp.int32, (slots, span), 0) == slot_of
    row_of = lax.broadcasted_iota(jnp.int32, (kept, span), 1) % tile_rows
    row = lax.broadcasted_iota(jnp.int32, (kept, span), 0)
    row_is = row % tile_rows == row_of
    wanted = (row // tile_rows + 1).astype(jnp.float32)

    def add_sources(first):
        codes = jnp.concatenate(
            [wide[pl.ds(first * rows + base + CAP * tile_rows + c, few, stride=rows), :] for c in range(CAP)], axis=0
        )
        across = jnp.concatenate([codes] * (span // LANES), axis=1)
        across = jnp.sum(jnp.where(slot_is, across, 0.0), axis=0, keepdims=True)
        landing = jnp.where(row_is & (across == wanted), 1.0, 0.0).astype(jnp.bfloat16)
        tiles = [
            wide[pl.ds((first + q) * rows + base + c * tile_rows, tile_rows), :].astype(jnp.bfloat16)
            for c in range(CAP)
            for q in range(few)
        ]
        counts = [
            jnp.sum(jnp.where(codes == k + 1.0, 1.0, 0.0), axis=0, keepdims=True) for k in range(n_tiles)
        ]
        return dot(landing, jnp.concatenate(tiles, axis=0)), counts

    total, counts = add_sources(0)
    if few < n_devices:
        sums[...] = total

        def add_more(n, counts):
            total, more = add_sources(n * few)
            sums[...] = sums[...] + total
            return tuple(a + b for a, b in zip(counts, more))

        counts = lax.fori_loop(1, n_devices // few, add_more, tuple(counts))
        total = sums[...]
    lhs = jnp.concatenate(
        [
            jnp.concatenate(
                [wide[pl.ds(t * right_rows + g, n_devices, stride=rows), :] for t in range(lines)], axis=0
            ).astype(jnp.bfloat16)
            for g in range(right_rows)
        ],
        axis=1,
    )
    outer = dot(lhs, folded[...])
    order = exchange_order(n_devices)
    for i in range(lines):
        for t in range(lines):
            part = outer[t * n_devices : (t + 1) * n_devices, i * pair_chan : (i + 1) * pair_chan]
            if order == tuple(range(n_devices)):
                opm[pl.ds(i * n_tokens + t, n_devices, stride=lines), :] = part
            else:
                for q, d in enumerate(order):
                    opm[pl.ds(i * n_tokens + d * lines + t, 1), :] = part[q : q + 1]
    packed = LANES // n_temp
    per_row = tile_rows // lines
    for k in range(n_tiles):
        at = pl.ds(k * tile_rows, tile_rows)
        mean = total[k * tile_rows : (k + 1) * tile_rows] / jnp.maximum(counts[k], 1.0)
        template = (mean * same_ref[at, :]).astype(jnp.bfloat16)
        for h in range(packed):
            part = dot(template[:, h * n_temp : (h + 1) * n_temp], structural)
            for i in range(lines):
                first = i * n_tokens + k * tc + h
                pair[pl.ds(first, per_row, stride=packed), :] = part[i * per_row : (i + 1) * per_row]
    for i in range(lines):
        at = pl.ds(i * n_tokens, n_tokens)
        total = pair[at, :] + (opm[at, :] + offset_ref[...].astype(jnp.float32))
        pair_normed = standardize(total).astype(jnp.bfloat16)
        gate = jax.nn.sigmoid(dot(pair_normed, sigmoid))
        linear = dot(pair_normed, content)
        out_ref[at, :] = (gate * linear).astype(out_ref.dtype)


def grant(*arrays):
    return pltpu.CompilerParams(
        vmem_limit_bytes=sum(2 * math.prod(shape) * jnp.dtype(kind).itemsize for shape, kind in arrays) + (1 << 20)
    )


def on_device(
    aligned_sequences,
    first_factor_matrix,
    second_factor_matrix,
    tensor_matrix,
    tensor_offset,
    structural_duplex_patches,
    patch_source_index,
    patch_target_index,
    structural_matrix,
    polymer_residue_lengths,
    sigmoid_matrix,
    content_matrix,
):
    n_devices = lax.axis_size("row")
    depth, lines, n_feat = aligned_sequences.shape
    slots, width = structural_duplex_patches.shape
    n_chan = first_factor_matrix.shape[1]
    n_temp, pair_chan = structural_matrix.shape
    tc = width // (lines * n_temp)
    n_tokens = lines * n_devices
    n_tiles = n_tokens // tc
    tile_rows = width // LANES
    right_rows = n_chan * depth // LANES
    rows = lines * right_rows + CAP * tile_rows + CAP
    vmem = pl.BlockSpec(memory_space=VMEM)
    hbm = pl.BlockSpec(memory_space=HBM)
    half = n_chan // 2
    f32, bf16, i32 = jnp.float32, jnp.bfloat16, jnp.int32

    arguments = (
        aligned_sequences.reshape(depth * lines, n_feat),
        second_factor_matrix.T,
        structural_duplex_patches,
        patch_source_index.reshape(1, slots),
        patch_target_index.reshape(1, slots),
        first_factor_matrix.T,
        polymer_residue_lengths,
        tensor_matrix.reshape(n_chan, half, 2, pair_chan),
        tensor_offset.reshape(1, pair_chan),
        structural_matrix,
        sigmoid_matrix,
        content_matrix,
    )
    results = (
        ((n_devices * rows, LANES), bf16),
        ((2 * lines * depth, 2 * n_chan), bf16),
        ((n_tiles * tile_rows, LANES), f32),
        ((half, n_chan, 2, pair_chan), bf16),
        ((1, pair_chan), bf16),
        ((n_temp + 2 * pair_chan, pair_chan), bf16),
    )
    scratch = (
        ((depth * lines + 2 * n_chan, n_feat), bf16),
        ((slots, width), bf16),
        ((2, slots), i32),
    )
    packed_wide = ((n_devices * rows, LANES), f32)
    send, left, same, tensor, offset, weights = pl.pallas_call(
        functools.partial(pack_kernel, n_devices, lines, rows, tc),
        out_shape=[jax.ShapeDtypeStruct(*r) for r in results],
        in_specs=[hbm] * len(arguments),
        out_specs=[vmem] * len(results),
        scratch_shapes=[pltpu.VMEM(*a) for a in scratch]
        + [pltpu.SMEM(polymer_residue_lengths.shape, i32), pltpu.VMEM((depth * lines, n_feat), f32)]
        + [pltpu.VMEM(*packed_wide)]
        + [pltpu.SemaphoreType.DMA((7,))],
        compiler_params=grant(*results, *scratch, packed_wide),
    )(*(pltpu.with_memory_space_constraint(a, HBM) for a in arguments))
    got = lax.all_to_all(
        send.reshape(n_devices, rows // 2, 2, LANES),
        "row",
        split_axis=0,
        concat_axis=0,
        tiled=True,
        axis_index_groups=[exchange_order(n_devices)],
    ).reshape(n_devices * rows, LANES)
    tensor = tensor.reshape(n_chan * n_chan, pair_chan)
    scratch = (
        ((n_chan * depth, lines * pair_chan), bf16),
        packed_wide,
        ((n_tiles * tile_rows, LANES), f32),
        ((lines * n_tokens, pair_chan), f32),
        ((lines * n_tokens, pair_chan), f32),
    )
    result = ((lines * n_tokens, pair_chan), bf16)
    out = pl.pallas_call(
        functools.partial(pair_kernel, n_devices, rows, tc),
        out_shape=jax.ShapeDtypeStruct(*result),
        in_specs=[vmem] * 6,
        out_specs=vmem,
        scratch_shapes=[pltpu.VMEM(*a) for a in scratch],
        compiler_params=grant(*results, *scratch, result),
    )(got, left, same, tensor, offset, weights)
    return out.reshape(lines, n_tokens, pair_chan)


def solution(mesh):
    placed = (
        P(None, ("grp", "row"), None),
        P(),
        P(),
        P(),
        P(),
        P(("grp", "row"), None),
        P(("grp", "row"), None),
        P(("grp", "row")),
        P(),
        P("grp"),
        P(),
        P(),
    )
    return jax.shard_map(
        on_device,
        mesh=mesh,
        in_specs=placed,
        out_specs=P(("grp", "row"), None, None),
        check_vma=False,
    )
```

time: 16.1 us -> 15.6 us (0.969)
  Pallas kernels: 3.37 us -> 2.89 us
    pallas_call x1, Pallas kernels: 1.88 us -> 1.4 us  [on_device(): pl.pallas_call(functools.partial(pack_kernel, n_devices, lines, rows, tc)...]
where the time goes in v1:
time: 15.6 us; the launch traced here: 15.3 us
  blocking collectives  12.4 us (79%)
  Pallas kernels  2.89 us (19%)
    all_to_all x1, blocking collectives, on_device(): lax.all_to_all(send.reshape(n_devices, rows // 2, 2, LANES), 'row', split...  12.4 us
    pallas_call x1, Pallas kernels, on_device(): pl.pallas_call(functools.partial(pair_kernel, n_devices, rows, tc), out_s...  1.49 us
    pallas_call x1, Pallas kernels, on_device(): pl.pallas_call(functools.partial(pack_kernel, n_devices, lines, rows, tc)...  1.4 us

profile of v1, /device:TPU:0, one launch (start us, length us, event | category | flops | bytes accessed | tf_op | source)
XLA Modules:
  0.0 15.3 jit_solution(1326500923643588043)
XLA Ops:
  0.0 1.4 %shard_map.118 = (bf16[800,128]{1,0:T(8,128)(2,1)S(1)}, bf16[128,64]{1,0:T(8,128)(2,1)S(1)}, f32[32,128]{1,0:T(8,128)S(1)}, bf16[16,32,2,128]{3,2,1,0:T(2,128)(2...) custom-call(bf16[64,64]{1,0:T(8,128)(2,1)} %bitcast.15, bf16[32,64]{1,0:T(8,128)(2,1)} %bitcast.16, ...), custom_call_target="tpu_custom_call" | custom-call | tf_op jit(solution)/shard_map/pallas_call | solution.py:356
  1.4 12.4 %all_to_all.5 = bf16[16,25,2,128]{3,2,1,0:T(2,128)(2,1)S(1)} all-to-all(bf16[16,25,2,128]{3,2,1,0:T(2,128)(2,1)S(1)} %bitcast.13), channel_id=1, replica_groups={{8,3,5,2,15,7,12,4,14,13,10,1,6,11,0,9},{24,19,21,18,31,23,28,20,30,29,..., dimensions={0} | all-to-all | bytes 409600 | tf_op jit(solution)/shard_map/all_to_all | solution.py:367
  13.8 1.5 %shard_map.119 = bf16[64,128]{1,0:T(8,128)(2,1)} custom-call(bf16[800,128]{1,0:T(8,128)(2,1)S(1)} %bitcast.11, bf16[128,64]{1,0:T(8,128)(2,1)S(1)} %get-tuple-element.12.left_ref, f32[32,128]{1,0:T(8,128)S(1)} %get-tuple-element.13.same_ref, bf16[1024,128]{1,0:T(8,128)(2,1)S(1)} %bitcast.12, bf16[1,128]{1,0:T(2,128)(2,1)S(1)} %get-tuple-element.15.offset_ref, ...), custom_call_target="tpu_custom_call" | custom-call | tf_op jit(solution)/shard_map/pallas_call | solution.py:384

commit v2 on v1

--- a/solution.py
+++ b/solution.py
@@ -179,15 +179,14 @@
     wide,
     sums,
     pair,
-    opm,
 ):
     pair_chan = weights_ref.shape[1]
     n_temp = weights_ref.shape[0] - 2 * pair_chan
     structural = weights_ref[pl.ds(0, n_temp), :]
     sigmoid = weights_ref[pl.ds(n_temp, pair_chan), :]
     content = weights_ref[pl.ds(n_temp + pair_chan, pair_chan), :]
-    lines = folded.shape[1] // pair_chan
-    right_rows = folded.shape[0] // LANES
+    lines = folded.shape[0]
+    right_rows = folded.shape[1] // LANES
     depth = left_ref.shape[0] // (2 * lines)
     n_tokens = n_devices * lines
     n_tiles = n_tokens // tc
@@ -195,20 +194,23 @@
     base = lines * right_rows
 
     width = left_ref.shape[1]
-    for p in range(0, tensor_ref.shape[0] // width, 2):
-        both = jnp.concatenate(
-            [tensor_ref[pl.ds(p * width, width), :], tensor_ref[pl.ds((p + 1) * width, width), :]], axis=1
-        )
-        part = dot(left_ref[...], both).astype(jnp.bfloat16)
-        for n in range(2):
-            for parity in range(2):
-                d = 2 * (p + n) + parity
-                at = (d % right_rows) * LANES + (d // right_rows) * depth
-                for t in range(lines):
-                    first = (parity * lines + t) * depth
-                    folded[pl.ds(at, depth), t * pair_chan : (t + 1) * pair_chan] = part[
-                        first : first + depth, n * pair_chan : (n + 1) * pair_chan
-                    ]
+    chans = tensor_ref.shape[0] // width
+    half = right_rows // 2
+    for p0 in range(half):
+        for p in range(p0, chans, 2 * half):
+            both = jnp.concatenate(
+                [tensor_ref[pl.ds(p * width, width), :], tensor_ref[pl.ds((p + half) * width, width), :]], axis=1
+            )
+            part = dot(left_ref[...], both).astype(jnp.bfloat16)
+            for n in range(2):
+                for parity in range(2):
+                    d = 2 * (p + n * half) + parity
+                    at = (d % right_rows) * LANES + (d // right_rows) * depth
+                    for t in range(lines):
+                        first = (parity * lines + t) * depth
+                        folded[t, pl.ds(at, depth), :] = part[
+                            first : first + depth, n * pair_chan : (n + 1) * pair_chan
+                        ]
 
     wide[...] = got_ref[...].astype(jnp.float32)
     few = min(n_devices, 16)
@@ -259,16 +261,25 @@
         ],
         axis=1,
     )
-    outer = dot(lhs, folded[...])
     order = exchange_order(n_devices)
-    for i in range(lines):
-        for t in range(lines):
-            part = outer[t * n_devices : (t + 1) * n_devices, i * pair_chan : (i + 1) * pair_chan]
-            if order == tuple(range(n_devices)):
-                opm[pl.ds(i * n_tokens + t, n_devices, stride=lines), :] = part
-            else:
-                for q, d in enumerate(order):
-                    opm[pl.ds(i * n_tokens + d * lines + t, 1), :] = part[q : q + 1]
+    token = lax.broadcasted_iota(jnp.int32, (n_tokens, n_tokens), 0)
+    held = lax.broadcasted_iota(jnp.int32, (n_tokens, n_tokens), 1)
+    position = held % n_devices
+    device = position
+    if order != tuple(range(n_devices)):
+        device = jnp.zeros_like(held)
+        for p, d in enumerate(order):
+            device = jnp.where(position == p, d, device)
+    swap = (token == device * lines + held // n_devices).astype(jnp.bfloat16)
+    lhs = dot(swap, lhs).astype(jnp.bfloat16)
+    outer = None
+    step = folded.shape[1] // 2
+    for at in range(0, folded.shape[1], step):
+        term = dot(
+            lhs[:, at : at + step],
+            jnp.concatenate([folded[i, pl.ds(at, step), :] for i in range(lines)], axis=1),
+        )
+        outer = term if outer is None else outer + term
     packed = LANES // n_temp
     per_row = tile_rows // lines
     for k in range(n_tiles):
@@ -282,7 +293,9 @@
                 pair[pl.ds(first, per_row, stride=packed), :] = part[i * per_row : (i + 1) * per_row]
     for i in range(lines):
         at = pl.ds(i * n_tokens, n_tokens)
-        total = pair[at, :] + (opm[at, :] + offset_ref[...].astype(jnp.float32))
+        total = pair[at, :] + (
+            outer[:, i * pair_chan : (i + 1) * pair_chan] + offset_ref[...].astype(jnp.float32)
+        )
         pair_normed = standardize(total).astype(jnp.bfloat16)
         gate = jax.nn.sigmoid(dot(pair_normed, sigmoid))
         linear = dot(pair_normed, content)
@@ -374,10 +387,9 @@
     ).reshape(n_devices * rows, LANES)
     tensor = tensor.reshape(n_chan * n_chan, pair_chan)
     scratch = (
-        ((n_chan * depth, lines * pair_chan), bf16),
+        ((lines, n_chan * depth, pair_chan), bf16),
         packed_wide,
         ((n_tiles * tile_rows, LANES), f32),
-        ((lines * n_tokens, pair_chan), f32),
         ((lines * n_tokens, pair_chan), f32),
     )
     result = ((lines * n_tokens, pair_chan), bf16)

time: 15.6 us -> 15.6 us (level)
  no operation moved by 1% of the time
where the time goes in v2:
time: 15.6 us; the launch traced here: 15.3 us
  blocking collectives  12.4 us (79%)
  Pallas kernels  2.87 us (18%)
    all_to_all x1, blocking collectives, on_device(): lax.all_to_all(send.reshape(n_devices, rows // 2, 2, LANES), 'row', split...  12.4 us
    pallas_call x1, Pallas kernels, on_device(): pl.pallas_call(functools.partial(pair_kernel, n_devices, rows, tc), out_s...  1.47 us
    pallas_call x1, Pallas kernels, on_device(): pl.pallas_call(functools.partial(pack_kernel, n_devices, lines, rows, tc)...  1.4 us

profile of v2, /device:TPU:0, one launch (start us, length us, event | category | flops | bytes accessed | tf_op | source)
XLA Modules:
  0.0 15.3 jit_solution(17330397841375805717)
XLA Ops:
  0.0 1.4 %shard_map.118 = (bf16[800,128]{1,0:T(8,128)(2,1)S(1)}, bf16[128,64]{1,0:T(8,128)(2,1)S(1)}, f32[32,128]{1,0:T(8,128)S(1)}, bf16[16,32,2,128]{3,2,1,0:T(2,128)(2...) custom-call(bf16[64,64]{1,0:T(8,128)(2,1)} %bitcast.15, bf16[32,64]{1,0:T(8,128)(2,1)} %bitcast.16, ...), custom_call_target="tpu_custom_call" | custom-call | tf_op jit(solution)/shard_map/pallas_call | solution.py:369
  1.4 12.4 %all_to_all.5 = bf16[16,25,2,128]{3,2,1,0:T(2,128)(2,1)S(1)} all-to-all(bf16[16,25,2,128]{3,2,1,0:T(2,128)(2,1)S(1)} %bitcast.13), channel_id=1, replica_groups={{8,3,5,2,15,7,12,4,14,13,10,1,6,11,0,9},{24,19,21,18,31,23,28,20,30,29,..., dimensions={0} | all-to-all | bytes 409600 | tf_op jit(solution)/shard_map/all_to_all | solution.py:380
  13.8 1.5 %shard_map.119 = bf16[64,128]{1,0:T(8,128)(2,1)} custom-call(bf16[800,128]{1,0:T(8,128)(2,1)S(1)} %bitcast.11, bf16[128,64]{1,0:T(8,128)(2,1)S(1)} %get-tuple-element.12.left_ref, f32[32,128]{1,0:T(8,128)S(1)} %get-tuple-element.13.same_ref, bf16[1024,128]{1,0:T(8,128)(2,1)S(1)} %bitcast.12, bf16[1,128]{1,0:T(2,128)(2,1)S(1)} %get-tuple-element.15.offset_ref, ...), custom_call_target="tpu_custom_call" | custom-call | tf_op jit(solution)/shard_map/pallas_call | solution.py:396

commit v3 on v2

--- a/solution.py
+++ b/solution.py
@@ -10,7 +10,7 @@
 
 CAP = 2
 LANES = 128
-ORDERS = {16: (8, 3, 5, 2, 15, 7, 12, 4, 14, 13, 10, 1, 6, 11, 0, 9)}
+ORDERS = {16: (11, 0, 9, 8, 15, 5, 3, 1, 7, 12, 4, 14, 13, 10, 2, 6)}
 VMEM = pltpu.MemorySpace.VMEM
 HBM = pltpu.MemorySpace.HBM
 

time: 15.6 us -> 15.3 us (0.981)
  blocking collectives: 12.4 us -> 12.2 us
    all_to_all x1, blocking collectives: 12.4 us -> 12.2 us  [on_device(): lax.all_to_all(send.reshape(n_devices, rows // 2, 2, LANES), 'row', split...]
where the time goes in v3:
time: 15.3 us; the launch traced here: 15.1 us
  blocking collectives  12.2 us (80%)
  Pallas kernels  2.87 us (19%)
    all_to_all x1, blocking collectives, on_device(): lax.all_to_all(send.reshape(n_devices, rows // 2, 2, LANES), 'row', split...  12.2 us
    pallas_call x1, Pallas kernels, on_device(): pl.pallas_call(functools.partial(pair_kernel, n_devices, rows, tc), out_s...  1.47 us
    pallas_call x1, Pallas kernels, on_device(): pl.pallas_call(functools.partial(pack_kernel, n_devices, lines, rows, tc)...  1.4 us

profile of v3, /device:TPU:0, one launch (start us, length us, event | category | flops | bytes accessed | tf_op | source)
XLA Modules:
  0.0 15.1 jit_solution(8037372796271638779)
XLA Ops:
  0.0 1.4 %shard_map.118 = (bf16[800,128]{1,0:T(8,128)(2,1)S(1)}, bf16[128,64]{1,0:T(8,128)(2,1)S(1)}, f32[32,128]{1,0:T(8,128)S(1)}, bf16[16,32,2,128]{3,2,1,0:T(2,128)(2...) custom-call(bf16[64,64]{1,0:T(8,128)(2,1)} %bitcast.15, bf16[32,64]{1,0:T(8,128)(2,1)} %bitcast.16, ...), custom_call_target="tpu_custom_call" | custom-call | tf_op jit(solution)/shard_map/pallas_call | solution.py:369
  1.4 12.2 %all_to_all.5 = bf16[16,25,2,128]{3,2,1,0:T(2,128)(2,1)S(1)} all-to-all(bf16[16,25,2,128]{3,2,1,0:T(2,128)(2,1)S(1)} %bitcast.13), channel_id=1, replica_groups={{11,0,9,8,15,5,3,1,7,12,4,14,13,10,2,6},{27,16,25,24,31,21,19,17,23,28,..., dimensions={0} | all-to-all | bytes 409600 | tf_op jit(solution)/shard_map/all_to_all | solution.py:380
  13.6 1.5 %shard_map.119 = bf16[64,128]{1,0:T(8,128)(2,1)} custom-call(bf16[800,128]{1,0:T(8,128)(2,1)S(1)} %bitcast.11, bf16[128,64]{1,0:T(8,128)(2,1)S(1)} %get-tuple-element.12.left_ref, f32[32,128]{1,0:T(8,128)S(1)} %get-tuple-element.13.same_ref, bf16[1024,128]{1,0:T(8,128)(2,1)S(1)} %bitcast.12, bf16[1,128]{1,0:T(2,128)(2,1)S(1)} %get-tuple-element.15.offset_ref, ...), custom_call_target="tpu_custom_call" | custom-call | tf_op jit(solution)/shard_map/pallas_call | solution.py:396

commit v4 on v3

--- a/solution.py
+++ b/solution.py
@@ -10,7 +10,7 @@
 
 CAP = 2
 LANES = 128
-ORDERS = {16: (11, 0, 9, 8, 15, 5, 3, 1, 7, 12, 4, 14, 13, 10, 2, 6)}
+ORDERS = {16: (11, 0, 2, 8, 5, 7, 3, 1, 13, 14, 4, 12, 15, 10, 9, 6)}
 VMEM = pltpu.MemorySpace.VMEM
 HBM = pltpu.MemorySpace.HBM
 
@@ -122,6 +122,13 @@
         wide[pl.ds(base + CAP * tile_rows + c, n_devices, stride=rows), :] = code[
             c * n_devices : (c + 1) * n_devices
         ]
+    place = place.astype(jnp.bfloat16)
+    placed = dot(place, tiles_ref[...])
+    for q in range(tile_rows):
+        for c in range(CAP):
+            wide[pl.ds(base + c * tile_rows + q, n_devices, stride=rows), :] = placed[
+                c * n_devices : (c + 1) * n_devices, q * LANES : (q + 1) * LANES
+            ]
     height = lines * depth
     normed_ref[...] = standardize(features_ref[pl.ds(0, height), :].astype(jnp.float32))
     second = features_ref[pl.ds(height, n_chan), :]
@@ -139,13 +146,6 @@
             left = dot_nt(normed, first[parity * 2 * n_chan : (parity + 1) * 2 * n_chan])
             left = left.astype(jnp.bfloat16).astype(jnp.float32) * (1.0 / depth)
             left_ref[pl.ds((parity * lines + t) * depth, depth), :] = left.astype(jnp.bfloat16)
-    place = place.astype(jnp.bfloat16)
-    for q in range(tile_rows):
-        placed = dot(place, tiles_ref[:, q * LANES : (q + 1) * LANES])
-        for c in range(CAP):
-            wide[pl.ds(base + c * tile_rows + q, n_devices, stride=rows), :] = placed[
-                c * n_devices : (c + 1) * n_devices
-            ]
     low = jnp.zeros_like(column)
     high = jnp.zeros_like(column)
     for i in range(lines):

time: 15.3 us -> 15 us (0.980)
  the two profiles are of different devices: /device:TPU:0 before, /device:TPU:6 now
where the time goes in v4:
time: 15 us; the launch traced here: 14.8 us
  blocking collectives  11.9 us (79%)
  Pallas kernels  2.96 us (20%)
    all_to_all x1, blocking collectives, on_device(): lax.all_to_all(send.reshape(n_devices, rows // 2, 2, LANES), 'row', split...  11.9 us
    pallas_call x1, Pallas kernels, on_device(): pl.pallas_call(functools.partial(pack_kernel, n_devices, lines, rows, tc)...  1.48 us
    pallas_call x1, Pallas kernels, on_device(): pl.pallas_call(functools.partial(pair_kernel, n_devices, rows, tc), out_s...  1.48 us

profile of v4, /device:TPU:6, one launch (start us, length us, event | category | flops | bytes accessed | tf_op | source)
XLA Modules:
  0.0 14.8 jit_solution(17587706211110847551)
XLA Ops:
  0.0 1.5 %shard_map.118 = (bf16[800,128]{1,0:T(8,128)(2,1)S(1)}, bf16[128,64]{1,0:T(8,128)(2,1)S(1)}, f32[32,128]{1,0:T(8,128)S(1)}, bf16[16,32,2,128]{3,2,1,0:T(2,128)(2...) custom-call(bf16[64,64]{1,0:T(8,128)(2,1)} %bitcast.15, bf16[32,64]{1,0:T(8,128)(2,1)} %bitcast.16, ...), custom_call_target="tpu_custom_call" | custom-call | tf_op jit(solution)/shard_map/pallas_call | solution.py:369
  1.5 11.9 %all_to_all.5 = bf16[16,25,2,128]{3,2,1,0:T(2,128)(2,1)S(1)} all-to-all(bf16[16,25,2,128]{3,2,1,0:T(2,128)(2,1)S(1)} %bitcast.13), channel_id=1, replica_groups={{11,0,2,8,5,7,3,1,13,14,4,12,15,10,9,6},{27,16,18,24,21,23,19,17,29,30,..., dimensions={0} | all-to-all | bytes 409600 | tf_op jit(solution)/shard_map/all_to_all | solution.py:380
  13.3 1.5 %shard_map.119 = bf16[64,128]{1,0:T(8,128)(2,1)} custom-call(bf16[800,128]{1,0:T(8,128)(2,1)S(1)} %bitcast.11, bf16[128,64]{1,0:T(8,128)(2,1)S(1)} %get-tuple-element.12.left_ref, f32[32,128]{1,0:T(8,128)S(1)} %get-tuple-element.13.same_ref, bf16[1024,128]{1,0:T(8,128)(2,1)S(1)} %bitcast.12, bf16[1,128]{1,0:T(2,128)(2,1)S(1)} %get-tuple-element.15.offset_ref, ...), custom_call_target="tpu_custom_call" | custom-call | tf_op jit(solution)/shard_map/pallas_call | solution.py:396

commit v5 on v3

--- a/solution.py
+++ b/solution.py
@@ -10,7 +10,7 @@
 
 CAP = 2
 LANES = 128
-ORDERS = {16: (11, 0, 9, 8, 15, 5, 3, 1, 7, 12, 4, 14, 13, 10, 2, 6)}
+ORDERS = {16: (11, 0, 2, 8, 5, 7, 3, 1, 15, 14, 4, 12, 13, 10, 9, 6)}
 VMEM = pltpu.MemorySpace.VMEM
 HBM = pltpu.MemorySpace.HBM
 

time: 15.3 us -> 14.9 us (0.974)
  blocking collectives: 12.2 us -> 11.8 us
    all_to_all x1, blocking collectives: 12.2 us -> 11.8 us  [on_device(): lax.all_to_all(send.reshape(n_devices, rows // 2, 2, LANES), 'row', split...]
where the time goes in v5:
time: 14.9 us; the launch traced here: 14.7 us
  blocking collectives  11.8 us (79%)
  Pallas kernels  2.87 us (19%)
    all_to_all x1, blocking collectives, on_device(): lax.all_to_all(send.reshape(n_devices, rows // 2, 2, LANES), 'row', split...  11.8 us
    pallas_call x1, Pallas kernels, on_device(): pl.pallas_call(functools.partial(pair_kernel, n_devices, rows, tc), out_s...  1.47 us
    pallas_call x1, Pallas kernels, on_device(): pl.pallas_call(functools.partial(pack_kernel, n_devices, lines, rows, tc)...  1.4 us

profile of v5, /device:TPU:0, one launch (start us, length us, event | category | flops | bytes accessed | tf_op | source)
XLA Modules:
  0.0 14.7 jit_solution(10912199266594034072)
XLA Ops:
  0.0 1.4 %shard_map.118 = (bf16[800,128]{1,0:T(8,128)(2,1)S(1)}, bf16[128,64]{1,0:T(8,128)(2,1)S(1)}, f32[32,128]{1,0:T(8,128)S(1)}, bf16[16,32,2,128]{3,2,1,0:T(2,128)(2...) custom-call(bf16[64,64]{1,0:T(8,128)(2,1)} %bitcast.15, bf16[32,64]{1,0:T(8,128)(2,1)} %bitcast.16, ...), custom_call_target="tpu_custom_call" | custom-call | tf_op jit(solution)/shard_map/pallas_call | solution.py:369
  1.4 11.8 %all_to_all.5 = bf16[16,25,2,128]{3,2,1,0:T(2,128)(2,1)S(1)} all-to-all(bf16[16,25,2,128]{3,2,1,0:T(2,128)(2,1)S(1)} %bitcast.13), channel_id=1, replica_groups={{11,0,2,8,5,7,3,1,15,14,4,12,13,10,9,6},{27,16,18,24,21,23,19,17,31,30,..., dimensions={0} | all-to-all | bytes 409600 | tf_op jit(solution)/shard_map/all_to_all | solution.py:380
  13.2 1.5 %shard_map.119 = bf16[64,128]{1,0:T(8,128)(2,1)} custom-call(bf16[800,128]{1,0:T(8,128)(2,1)S(1)} %bitcast.11, bf16[128,64]{1,0:T(8,128)(2,1)S(1)} %get-tuple-element.12.left_ref, f32[32,128]{1,0:T(8,128)S(1)} %get-tuple-element.13.same_ref, bf16[1024,128]{1,0:T(8,128)(2,1)S(1)} %bitcast.12, bf16[1,128]{1,0:T(2,128)(2,1)S(1)} %get-tuple-element.15.offset_ref, ...), custom_call_target="tpu_custom_call" | custom-call | tf_op jit(solution)/shard_map/pallas_call | solution.py:396

commit v6 on v5

--- a/solution.py
+++ b/solution.py
@@ -10,7 +10,7 @@
 
 CAP = 2
 LANES = 128
-ORDERS = {16: (11, 0, 2, 8, 5, 7, 3, 1, 15, 14, 4, 12, 13, 10, 9, 6)}
+ORDERS = {16: (11, 0, 9, 8, 2, 7, 3, 1, 13, 14, 4, 12, 5, 10, 15, 6)}
 VMEM = pltpu.MemorySpace.VMEM
 HBM = pltpu.MemorySpace.HBM
 

time: 14.9 us -> 14.9 us (level)
  the two profiles are of different devices: /device:TPU:0 before, /device:TPU:1 now
where the time goes in v6:
time: 14.9 us; the launch traced here: 14.7 us
  blocking collectives  11.8 us (79%)
  Pallas kernels  2.87 us (19%)
    all_to_all x1, blocking collectives, on_device(): lax.all_to_all(send.reshape(n_devices, rows // 2, 2, LANES), 'row', split...  11.8 us
    pallas_call x1, Pallas kernels, on_device(): pl.pallas_call(functools.partial(pair_kernel, n_devices, rows, tc), out_s...  1.47 us
    pallas_call x1, Pallas kernels, on_device(): pl.pallas_call(functools.partial(pack_kernel, n_devices, lines, rows, tc)...  1.4 us

profile of v6, /device:TPU:1, one launch (start us, length us, event | category | flops | bytes accessed | tf_op | source)
XLA Modules:
  0.0 14.7 jit_solution(2025385000006591985)
XLA Ops:
  0.0 1.4 %shard_map.118 = (bf16[800,128]{1,0:T(8,128)(2,1)S(1)}, bf16[128,64]{1,0:T(8,128)(2,1)S(1)}, f32[32,128]{1,0:T(8,128)S(1)}, bf16[16,32,2,128]{3,2,1,0:T(2,128)(2...) custom-call(bf16[64,64]{1,0:T(8,128)(2,1)} %bitcast.15, bf16[32,64]{1,0:T(8,128)(2,1)} %bitcast.16, ...), custom_call_target="tpu_custom_call" | custom-call | tf_op jit(solution)/shard_map/pallas_call | solution.py:369
  1.4 11.8 %all_to_all.5 = bf16[16,25,2,128]{3,2,1,0:T(2,128)(2,1)S(1)} all-to-all(bf16[16,25,2,128]{3,2,1,0:T(2,128)(2,1)S(1)} %bitcast.13), channel_id=1, replica_groups={{11,0,9,8,2,7,3,1,13,14,4,12,5,10,15,6},{27,16,25,24,18,23,19,17,29,30,..., dimensions={0} | all-to-all | bytes 409600 | tf_op jit(solution)/shard_map/all_to_all | solution.py:380
  13.2 1.5 %shard_map.119 = bf16[64,128]{1,0:T(8,128)(2,1)} custom-call(bf16[800,128]{1,0:T(8,128)(2,1)S(1)} %bitcast.11, bf16[128,64]{1,0:T(8,128)(2,1)S(1)} %get-tuple-element.12.left_ref, f32[32,128]{1,0:T(8,128)S(1)} %get-tuple-element.13.same_ref, bf16[1024,128]{1,0:T(8,128)(2,1)S(1)} %bitcast.12, bf16[1,128]{1,0:T(2,128)(2,1)S(1)} %get-tuple-element.15.offset_ref, ...), custom_call_target="tpu_custom_call" | custom-call | tf_op jit(solution)/shard_map/pallas_call | solution.py:396
